TPU v7x, 256 devices: a whole 4x4x8 slice. The times are simulated.
256 devices in a mesh: dp: 2 (over core), ctx: 128 (over z, y, x).
Axes of the slice: x: 4, y: 4, z: 8, core: 2. Of those that a mesh axis runs over, the one named last changes fastest.
Arguments:
- hidden: bfloat16 [4, 16384, 5376], P('dp', 'ctx'), parts along dimension 0, may hold values from -400 to 400
- queries: bfloat16 [4, 16384, 2048], P('dp', 'ctx'), parts along dimension 0, may hold values from -400 to 400
- input_gain: float32 [5376], replicated, may hold values from 0.1 to 1.9
- kv_weight: bfloat16 [5376, 2048], P('ctx'), may hold values from -0.078125 to 0.078125
- query_gain: float32 [128], replicated, may hold values from 1 to 2.5
- key_gain: float32 [128], replicated, may hold values from 1 to 2.5
Outputs:
- attended: bfloat16 [4, 16384, 2048], P('dp', 'ctx'), parts along dimension 0
There are 2 independent parts, one for each index of `dp`. A program takes and returns all parts, laid end to end along the dimension named above; an argument that names none is the same for every part. Nothing has to cross between parts.
All inputs are finite; a program needn't handle non-finite values.
Results may differ from a plain program's by a relative error of at most 0.012.
Values may be sent and summed in bfloat16 or wider, within the bound.
A program may use at most 128 MiB of HBM per device.

v0:
```python
import jax
import jax.numpy as jnp
from jax import lax
from jax.sharding import PartitionSpec as P

HD = 128
WINDOW = 1024


attn_scalar = 168.0
norm_eps = 1e-06


def from_behind(block, axis, distance):
    devices = range(lax.axis_size(axis))
    route = [(i - distance, i) for i in devices if i - distance in devices]
    return lax.ppermute(block, axis, route)


def rotary_tables(positions, head_width):
    half_width = head_width // 2
    exponent = 2.0 * jnp.arange(half_width, dtype=jnp.float32) / head_width
    inverse = jnp.power(10000.0, -exponent)
    angles = positions.astype(jnp.float32)[:, None] * inverse[None, :]
    return (jnp.cos(angles), jnp.sin(angles))


def rotate(heads, cos_table, sine_table):
    half_width = heads.shape[-1] // 2
    first = heads[..., :half_width]
    second = heads[..., half_width:]
    cos_part = cos_table[:, None, :]
    sine_part = sine_table[:, None, :]
    return jnp.concatenate(
        [first * cos_part - second * sine_part, second * cos_part + first * sine_part], axis=-1
    )


def head_norm(heads, gain):
    return heads * lax.rsqrt(jnp.mean(heads * heads, axis=-1, keepdims=True) + norm_eps) * gain


def body(hidden, queries, input_gain, kv_weight, query_gain, key_gain):
    seq_count, block_len, model_width = hidden.shape
    kv_width = kv_weight.shape[1]
    kv_half = kv_width // 2
    kv_heads = kv_half // HD
    query_heads = queries.shape[2] // HD
    group_size = query_heads // kv_heads
    span_blocks = WINDOW // block_len
    token_rows = seq_count * block_len
    hidden_f32 = hidden.astype(jnp.float32)
    normed = (
        hidden_f32
        * lax.rsqrt(jnp.mean(hidden_f32 * hidden_f32, axis=-1, keepdims=True) + norm_eps)
        * input_gain
    )
    normed = normed.astype(jnp.bfloat16).reshape(token_rows, model_width)
    projected = jnp.dot(
        normed,
        lax.all_gather(kv_weight, "ctx", axis=0, tiled=True),
        preferred_element_type=jnp.float32,
    )
    key_proj = projected[:, :kv_half]
    value_proj = projected[:, kv_half:]
    shard_index = lax.axis_index("ctx")
    positions = shard_index * block_len + jnp.arange(block_len, dtype=jnp.int32)
    cos_table, sine_table = rotary_tables(positions, HD)
    key_part = key_proj.reshape(seq_count, block_len, kv_heads, HD)
    key_part = rotate(head_norm(key_part, key_gain), cos_table, sine_table).astype(jnp.bfloat16)
    value_part = value_proj.reshape(seq_count, block_len, kv_half).astype(jnp.bfloat16)
    key_block = jnp.concatenate(
        [key_part.reshape(seq_count, block_len, kv_half), value_part], axis=2
    )
    query_part = queries.astype(jnp.float32).reshape(seq_count, block_len, query_heads, HD)
    query_part = (
        rotate(head_norm(query_part, query_gain), cos_table, sine_table) * attn_scalar ** (-0.5)
    ).astype(jnp.bfloat16)
    previous = from_behind(key_block, "ctx", 1)
    pieces = [previous]
    for offset in range(2, span_blocks + 1):
        pieces.append(from_behind(key_block, "ctx", offset))
    window_blocks = jnp.concatenate(pieces[::-1] + [key_block], axis=1)
    key_pos = (shard_index - span_blocks) * block_len + jnp.arange(
        (span_blocks + 1) * block_len, dtype=jnp.int32
    )
    allowed = (
        (key_pos[None, :] <= positions[:, None])
        & (key_pos[None, :] > positions[:, None] - WINDOW)
        & (key_pos[None, :] >= 0)
    )
    outputs = []
    for seq_index in range(seq_count):
        window_keys = window_blocks[seq_index, :, :kv_half].reshape(-1, kv_heads, HD)
        window_values = window_blocks[seq_index, :, kv_half:].reshape(-1, kv_heads, HD)
        query_block = query_part[seq_index].reshape(block_len, kv_heads, group_size, HD)
        scores = jnp.einsum(
            "qhgd,khd->hgqk", query_block, window_keys, preferred_element_type=jnp.float32
        )
        weights = jnp.where(allowed, jnp.exp(scores), 0.0)
        row_total = jnp.sum(weights, axis=-1)
        weighted = jnp.einsum(
            "hgqk,khd->qhgd",
            weights.astype(jnp.bfloat16),
            window_values,
            preferred_element_type=jnp.float32,
        )
        result = weighted / jnp.transpose(row_total, (2, 0, 1))[..., None]
        outputs.append(result.astype(jnp.bfloat16).reshape(block_len, query_heads * HD))
    return jnp.stack(outputs, axis=0)


def solution(mesh):
    return jax.shard_map(
        body,
        mesh=mesh,
        in_specs=(P("dp", "ctx", None), P("dp", "ctx", None), P(), P("ctx", None), P(), P()),
        out_specs=P("dp", "ctx", None),
        check_vma=False,
    )
```

profile of v0, /device:TPU:64, one launch (start us, length us, event | category | flops | bytes accessed | tf_op | source)
XLA Modules:
  0.0 528.8 jit_solution(4616291720321876393)
XLA Ops:
  6.5 0.7 all-gather.3.cloned.1.call-update
  7.3 1.5 copy.71
  8.7 0.0 copy-start.2
  8.8 0.6 fusion.15
  9.4 0.1 copy.50
  9.5 0.1 copy.51
  9.6 0.0 copy-start.1
  9.7 2.6 fusion.4
  12.2 0.3 multiply_cosine_fusion
  12.5 0.9 and_and_fusion
  13.4 2.2 fusion.6
  15.7 174.9 %all-gather.3.cloned.1.call-done = bf16[128,42,2048]{2,1,0:T(8,128)(2,1)} async-done(((bf16[1,42,2048]{2,1,0:T(8,128)(2,1)}), bf16[128,42,2048]{2,1,0:T(8,128)(2,1)}) %all-gather.3.cloned.1.call-update) | async-done | bytes 22020112 | tf_op jit(solution)/shard_map/all_gather | solution.py:61
  190.5 27.7 %reshape.131 = bf16[5376,2048]{1,0:T(8,128)(2,1)} reshape(bf16[128,42,2048]{2,1,0:T(8,128)(2,1)} %all-gather.3.cloned.1.call-done) | data formatting | bytes 44040192
  218.2 11.1 %fusion.35 = f32[256,2048]{1,0:T(8,128)S(1)} fusion(bf16[256,5376]{1,0:T(8,128)(2,1)} %bitcast.101, bf16[5376,2048]{1,0:T(8,128)(2,1)} %reshape.131), kind=kOutput, calls=%fused_computation.65 | convolution fusion | flops 5637144576 | bytes 26869760 | tf_op jit(solution)/shard_map/dot_general | solution.py:59
  229.3 0.1 slice_bitcast_fusion
  229.4 0.9 slice.71
  230.2 0.2 copy.70
  230.4 1.0 fusion.24
  231.4 1.6 copy.46
  233.0 1.3 add_rsqrt_fusion.1
  234.3 1.5 copy.47
  235.8 1.3 fusion.25
  237.0 0.5 subtract_convert_fusion
  237.5 0.3 pad_maximum_fusion.2
  237.8 0.4 copy.48
  238.2 1.3 copy.49
  239.5 0.1 pad_maximum_fusion
  239.6 4.9 collective-permute-start
  244.5 2.8 collective-permute-start.1
  247.3 1.4 fusion.16
  248.6 6.4 %collective-permute-start.2 = (bf16[2,128,2048]{1,2,0:T(8,128)(2,1)S(1)}, bf16[2,128,2048]{1,2,0:T(8,128)(2,1)S(1)}, u32[]{:S(2)}, u32[]{:S(2)}) collective-permute-start(bf16[2,128,2048]{1,2,0:T(8,128)(2,1)S(1)} %pad_maximum_fusion), channel_id=1, source_target_pairs={{0,6},{1,7},{2,8},{3,9},{4,10},{5,11},{6,12},{7,13},{8,14},{9,15},... | collective-permute-start | bytes 3145736 | tf_op jit(solution)/shard_map/ppermute | solution.py:17
  255.1 0.6 multiply_subtract_fusion
  255.7 3.4 collective-permute-start.3
  259.1 0.6 fusion.17
  259.7 3.1 collective-permute-start.4
  262.8 0.2 fusion.34
  263.0 0.1 copy.55
  263.2 0.1 copy.52
  263.3 72.2 %collective-permute-done = bf16[2,128,2048]{1,2,0:T(8,128)(2,1)S(1)} collective-permute-done((bf16[2,128,2048]{1,2,0:T(8,128)(2,1)S(1)}, bf16[2,128,2048]{1,2,0:T(8,128)(2,1)S(1)}, u32[]{:S(2)}, u32[]{:S(2)}) %collective-permute-start) | collective-permute-done | bytes 1048608 | tf_op jit(solution)/shard_map/ppermute | solution.py:17
  335.5 5.4 %collective-permute-start.5 = (bf16[2,128,2048]{1,2,0:T(8,128)(2,1)S(1)}, bf16[2,128,2048]{1,2,0:T(8,128)(2,1)S(1)}, u32[]{:S(2)}, u32[]{:S(2)}) collective-permute-start(bf16[2,128,2048]{1,2,0:T(8,128)(2,1)S(1)} %pad_maximum_fusion), channel_id=1, source_target_pairs={{0,3},{1,4},{2,5},{3,6},{4,7},{5,8},{6,9},{7,10},{8,11},{9,12},{10... | collective-permute-start | bytes 3145736 | tf_op jit(solution)/shard_map/ppermute | solution.py:17
  340.9 0.2 constant_dynamic-update-slice_fusion.8
  341.1 23.2 %collective-permute-start.6 = (bf16[2,128,2048]{1,2,0:T(8,128)(2,1)S(1)}, bf16[2,128,2048]{1,2,0:T(8,128)(2,1)S(1)}, u32[]{:S(2)}, u32[]{:S(2)}) collective-permute-start(bf16[2,128,2048]{1,2,0:T(8,128)(2,1)S(1)} %pad_maximum_fusion), channel_id=1, source_target_pairs={{0,2},{1,3},{2,4},{3,5},{4,6},{5,7},{6,8},{7,9},{8,10},{9,11},{10,... | collective-permute-start | bytes 3145736 | tf_op jit(solution)/shard_map/ppermute | solution.py:17
  364.3 0.2 constant_dynamic-update-slice_fusion.7
  364.6 34.9 %collective-permute-start.7 = (bf16[2,128,2048]{1,2,0:T(8,128)(2,1)S(1)}, bf16[2,128,2048]{1,2,0:T(8,128)(2,1)S(1)}, u32[]{:S(2)}, u32[]{:S(2)}) collective-permute-start(bf16[2,128,2048]{1,2,0:T(8,128)(2,1)S(1)} %pad_maximum_fusion), channel_id=1, source_target_pairs={{0,1},{1,2},{2,3},{3,4},{4,5},{5,6},{6,7},{7,8},{8,9},{9,10},{10,1... | collective-permute-start | bytes 3145736 | tf_op jit(solution)/shard_map/ppermute | solution.py:17
  399.5 0.2 constant_dynamic-update-slice_fusion.6
  399.7 32.0 %collective-permute-done.3 = bf16[2,128,2048]{1,2,0:T(8,128)(2,1)S(1)} collective-permute-done((bf16[2,128,2048]{1,2,0:T(8,128)(2,1)S(1)}, bf16[2,128,2048]{1,2,0:T(8,128)(2,1)S(1)}, u32[]{:S(2)}, u32[]{:S(2)}) %collective-permute-start.3) | collective-permute-done | bytes 1048608 | tf_op jit(solution)/shard_map/ppermute | solution.py:17
  431.8 0.2 constant_dynamic-update-slice_fusion.5
  432.0 8.6 %collective-permute-done.4 = bf16[2,128,2048]{1,2,0:T(8,128)(2,1)S(1)} collective-permute-done((bf16[2,128,2048]{1,2,0:T(8,128)(2,1)S(1)}, bf16[2,128,2048]{1,2,0:T(8,128)(2,1)S(1)}, u32[]{:S(2)}, u32[]{:S(2)}) %collective-permute-start.4) | collective-permute-done | bytes 1048608 | tf_op jit(solution)/shard_map/ppermute | solution.py:17
  440.6 0.2 constant_dynamic-update-slice_fusion.4
  440.9 13.0 %collective-permute-done.5 = bf16[2,128,2048]{1,2,0:T(8,128)(2,1)S(1)} collective-permute-done((bf16[2,128,2048]{1,2,0:T(8,128)(2,1)S(1)}, bf16[2,128,2048]{1,2,0:T(8,128)(2,1)S(1)}, u32[]{:S(2)}, u32[]{:S(2)}) %collective-permute-start.5) | collective-permute-done | bytes 1048608 | tf_op jit(solution)/shard_map/ppermute | solution.py:17
  453.8 0.2 constant_dynamic-update-slice_fusion.3
  454.1 44.2 %collective-permute-done.6 = bf16[2,128,2048]{1,2,0:T(8,128)(2,1)S(1)} collective-permute-done((bf16[2,128,2048]{1,2,0:T(8,128)(2,1)S(1)}, bf16[2,128,2048]{1,2,0:T(8,128)(2,1)S(1)}, u32[]{:S(2)}, u32[]{:S(2)}) %collective-permute-start.6) | collective-permute-done | bytes 1048608 | tf_op jit(solution)/shard_map/ppermute | solution.py:17
  498.3 0.2 constant_dynamic-update-slice_fusion.2
  498.5 1.8 collective-permute-done.7
  500.3 0.2 constant_dynamic-update-slice_fusion.1
  500.6 0.2 constant_dynamic-update-slice_fusion
  500.8 2.0 fusion.33
  502.9 1.4 fusion.36
  504.3 3.6 fusion
  508.0 4.2 divide_convert_fusion.1
  512.2 1.2 copy.58
  513.4 6.2 %divide_convert_fusion = bf16[128,8,2,128]{0,3,2,1:T(8,128)(2,1)} fusion(bf16[1152,8,128,1]{0,2,3,1:T(8,128)(2,1)S(1)} %bitcast.102, f32[8,1152,128,2]{2,1,3,0:T(8,128)} %copy-done, pred[128,1152]{0,1:T(8,128)(4,1)S(1)} %and_and_fusion, f32[128,8,2]{0,2,1:T(2,128)S(1)} %bitcast.111), kind=kOutput, calls=%fused_computation.35 | convolution fusion | flops 609222656 | bytes 12476416 | tf_op jit(solution)/shard_map/hgqk,khd->qhgd/dot_general | solution.py:102
  519.7 1.2 copy.59
  520.9 1.1 pad_maximum_fusion.1
  (14 shorter events, 0.1 us)
Async XLA Ops:
  6.5 184.0 %all-gather.3.cloned.1.call-start = ((), (), s32[]{:S(2)}) async-start(), calls=%async_computation | async-start | bytes 25362432 | tf_op jit(solution)/shard_map/all_gather | solution.py:61
  8.7 4.7 copy-start.2
  9.6 3.9 copy-start.1
  239.6 96.0 %collective-permute-start = (bf16[2,128,2048]{1,2,0:T(8,128)(2,1)S(1)}, bf16[2,128,2048]{1,2,0:T(8,128)(2,1)S(1)}, u32[]{:S(2)}, u32[]{:S(2)}) collective-permute-start(bf16[2,128,2048]{1,2,0:T(8,128)(2,1)S(1)} %pad_maximum_fusion), channel_id=1, source_target_pairs={{0,8},{1,9},{2,10},{3,11},{4,12},{5,13},{6,14},{7,15},{8,16},{9,17... | collective-permute-start | bytes 3145736 | tf_op jit(solution)/shard_map/ppermute | solution.py:17
  244.5 96.6 %collective-permute-start.1 = (bf16[2,128,2048]{1,2,0:T(8,128)(2,1)S(1)}, bf16[2,128,2048]{1,2,0:T(8,128)(2,1)S(1)}, u32[]{:S(2)}, u32[]{:S(2)}) collective-permute-start(bf16[2,128,2048]{1,2,0:T(8,128)(2,1)S(1)} %pad_maximum_fusion), channel_id=1, source_target_pairs={{0,7},{1,8},{2,9},{3,10},{4,11},{5,12},{6,13},{7,14},{8,15},{9,16}... | collective-permute-start | bytes 3145736 | tf_op jit(solution)/shard_map/ppermute | solution.py:17
  248.6 115.9 %collective-permute-start.2 = (bf16[2,128,2048]{1,2,0:T(8,128)(2,1)S(1)}, bf16[2,128,2048]{1,2,0:T(8,128)(2,1)S(1)}, u32[]{:S(2)}, u32[]{:S(2)}) collective-permute-start(bf16[2,128,2048]{1,2,0:T(8,128)(2,1)S(1)} %pad_maximum_fusion), channel_id=1, source_target_pairs={{0,6},{1,7},{2,8},{3,9},{4,10},{5,11},{6,12},{7,13},{8,14},{9,15},... | collective-permute-start | bytes 3145736 | tf_op jit(solution)/shard_map/ppermute | solution.py:17
  255.7 176.1 %collective-permute-start.3 = (bf16[2,128,2048]{1,2,0:T(8,128)(2,1)S(1)}, bf16[2,128,2048]{1,2,0:T(8,128)(2,1)S(1)}, u32[]{:S(2)}, u32[]{:S(2)}) collective-permute-start(bf16[2,128,2048]{1,2,0:T(8,128)(2,1)S(1)} %pad_maximum_fusion), channel_id=1, source_target_pairs={{0,5},{1,6},{2,7},{3,8},{4,9},{5,10},{6,11},{7,12},{8,13},{9,14},{... | collective-permute-start | bytes 3145736 | tf_op jit(solution)/shard_map/ppermute | solution.py:17
  259.7 180.9 %collective-permute-start.4 = (bf16[2,128,2048]{1,2,0:T(8,128)(2,1)S(1)}, bf16[2,128,2048]{1,2,0:T(8,128)(2,1)S(1)}, u32[]{:S(2)}, u32[]{:S(2)}) collective-permute-start(bf16[2,128,2048]{1,2,0:T(8,128)(2,1)S(1)} %pad_maximum_fusion), channel_id=1, source_target_pairs={{0,4},{1,5},{2,6},{3,7},{4,8},{5,9},{6,10},{7,11},{8,12},{9,13},{1... | collective-permute-start | bytes 3145736 | tf_op jit(solution)/shard_map/ppermute | solution.py:17
  335.5 118.3 %collective-permute-start.5 = (bf16[2,128,2048]{1,2,0:T(8,128)(2,1)S(1)}, bf16[2,128,2048]{1,2,0:T(8,128)(2,1)S(1)}, u32[]{:S(2)}, u32[]{:S(2)}) collective-permute-start(bf16[2,128,2048]{1,2,0:T(8,128)(2,1)S(1)} %pad_maximum_fusion), channel_id=1, source_target_pairs={{0,3},{1,4},{2,5},{3,6},{4,7},{5,8},{6,9},{7,10},{8,11},{9,12},{10... | collective-permute-start | bytes 3145736 | tf_op jit(solution)/shard_map/ppermute | solution.py:17
  341.1 157.2 %collective-permute-start.6 = (bf16[2,128,2048]{1,2,0:T(8,128)(2,1)S(1)}, bf16[2,128,2048]{1,2,0:T(8,128)(2,1)S(1)}, u32[]{:S(2)}, u32[]{:S(2)}) collective-permute-start(bf16[2,128,2048]{1,2,0:T(8,128)(2,1)S(1)} %pad_maximum_fusion), channel_id=1, source_target_pairs={{0,2},{1,3},{2,4},{3,5},{4,6},{5,7},{6,8},{7,9},{8,10},{9,11},{10,... | collective-permute-start | bytes 3145736 | tf_op jit(solution)/shard_map/ppermute | solution.py:17
  364.6 135.7 %collective-permute-start.7 = (bf16[2,128,2048]{1,2,0:T(8,128)(2,1)S(1)}, bf16[2,128,2048]{1,2,0:T(8,128)(2,1)S(1)}, u32[]{:S(2)}, u32[]{:S(2)}) collective-permute-start(bf16[2,128,2048]{1,2,0:T(8,128)(2,1)S(1)} %pad_maximum_fusion), channel_id=1, source_target_pairs={{0,1},{1,2},{2,3},{3,4},{4,5},{5,6},{6,7},{7,8},{8,9},{9,10},{10,1... | collective-permute-start | bytes 3145736 | tf_op jit(solution)/shard_map/ppermute | solution.py:17
  504.3 3.7 copy-start
Sparse Core Ops, SparseCore 0:
  11.0 179.4 all-gather.2
where the time goes:
time: 530 us; the launch traced here: 529 us
  waiting for transfers between devices  347 us (65%)
  starting transfers between devices  84 us (16%)
  local copies, waits for them, and re-layouts  42.1 us (8%)
  matrix products  26.6 us (5%)
  other arithmetic  14.9 us (3%)
  between operations  13.8 us (3%)
    all_gather x1, waiting for transfers between devices, body(): lax.all_gather(kv_weight, 'ctx', axis=0, tiled=True)  175 us
    ppermute x8, waiting for transfers between devices, from_behind(): return lax.ppermute(block, axis, route)  172 us
    ppermute x8, starting transfers between devices, from_behind(): return lax.ppermute(block, axis, route)  84 us
    unnamed x18, local copies, waits for them, and re-layouts  31.4 us
    dot_general x1, matrix products, body(): jnp.dot(normed, lax.all_gather(kv_weight, 'ctx', axis=0, tiled=True), pre...  11.1 us
  transfers between devices with their start and end apart: 9, of which 7 were waited for; matrix products, arithmetic and copies ran while one was open for 2% of the time, Pallas kernels for 0%

commit v1 on v0

v1 whole, which is shorter than its diff:
```python
import jax
import jax.numpy as jnp
from jax import lax
from jax.experimental import pallas as pl
from jax.experimental.pallas import tpu as pltpu
from jax.sharding import PartitionSpec as P

HD = 128
WINDOW = 1024
EPS = 1e-6
SCALE = 168.0 ** -0.5
NX, NY, NZ = 4, 4, 8
PLANE = NX * NY
SLABS = WINDOW // HD
MEMBERS = 8
ROWS_B, ROWS_C = 176, 160
BF = jnp.bfloat16
F32 = jnp.float32
MESH = pl.DeviceIdType.MESH


def head_rotary(head, gain, cos, sin):
    mean = jnp.mean(head * head, axis=-1, keepdims=True)
    unit = head * lax.rsqrt(mean + EPS) * gain
    return unit * cos + pltpu.roll(unit, 64, 1) * sin


def kernel(
    w_ref, h_ref, q_ref, gain_ref, qg_ref, kg_ref, cos_ref, sin_ref, o_ref,
    landing, wb, wc, xn, acc, kvs, kvb, qn, qb, ob,
    a_s, a_r, row_s, row_r, z_s, z_r, l_s, l_r, x_s, x_r,
    q_s, q_r, kv_s, kv_r, halo_s, o_s, o_r,
):
    c = lax.axis_index("dp")
    t = lax.axis_index("ctx")
    z = lax.div(t, PLANE)
    i = lax.rem(t, PLANE)
    y = lax.div(i, NX)
    x = lax.rem(i, NX)
    yh = lax.div(y, 2)
    yl = lax.rem(y, 2)
    block_len = cos_ref.shape[0]

    def chip(zz, yy, xx):
        return zz * PLANE + yy * NX + xx

    def step(v, d, n):
        return lax.rem(v + (d % n), n)

    sibling = (1 - c, t)
    pending = []

    def remote(src, dst, send, recv, device):
        return pltpu.make_async_remote_copy(
            src_ref=src, dst_ref=dst, send_sem=send, recv_sem=recv,
            device_id=device, device_id_type=MESH,
        )

    def push(src, dst, send, recv, device):
        copy = remote(src, dst, send, recv, device)
        copy.start()
        pending.append(copy)

    def arrived(region, recv):
        pltpu.make_async_copy(region, region, recv).wait()

    barrier = pltpu.get_barrier_semaphore()
    for r in range(1, 2 * PLANE):
        dev = (lax.rem(c + r % 2, 2), z * PLANE + lax.rem(i + r // 2, PLANE))
        pl.semaphore_signal(barrier, inc=1, device_id=dev, device_id_type=MESH)
    for d in (1, -1):
        pl.semaphore_signal(
            barrier, inc=1, device_id=(c, chip(step(z, d, NZ), y, x)), device_id_type=MESH
        )

    cos = cos_ref[...]
    sin = sin_ref[...]
    qg = qg_ref[...]
    kg = kg_ref[...]
    for s in range(2):
        for h in range(16):
            head = q_ref[s, :, h * HD:(h + 1) * HD].astype(F32)
            qn[s, :, h * HD:(h + 1) * HD] = (head_rotary(head, qg, cos, sin) * SCALE).astype(BF)

    pl.semaphore_wait(barrier, 2 * PLANE - 1 + 2)

    j = yl * NX + x
    for r in range(1, MEMBERS):
        peer = lax.rem(j + r, MEMBERS)
        pyl, px = lax.div(peer, NX), lax.rem(peer, NX)
        col = pl.multiple_of(pyl * 1024 + c * 512 + px * HD, HD)
        push(
            w_ref.at[:, pl.ds(col, HD)], landing.at[j], a_s.at[r], a_r.at[r],
            (c, chip(z, yh * 2 + pyl, px)),
        )
    col = pl.multiple_of(yl * 1024 + c * 512 + x * HD, HD)
    landing[j] = w_ref[:, pl.ds(col, HD)]

    def q_pieces(start):
        for k in range(8):
            for kk in range(2):
                low = lax.rem(i + k, 8)
                core = lax.rem(c + kk, 2)
                s = lax.div(low, 4)
                h = core * 4 + lax.rem(low, 4)
                src = qn.at[s, :, pl.ds(pl.multiple_of(h * 256, 256), 256)]
                dst = qb.at[i]
                dev = (core, z * PLANE + c * 8 + low)
                send, recv = q_s.at[k * 2 + kk], q_r.at[i]
                if k == 0 and kk == 0:
                    here = lax.div(i, 8) == c

                    @pl.when(here)
                    def _():
                        if start:
                            pltpu.make_async_copy(src, dst, recv).start()

                    @pl.when(jnp.logical_not(here))
                    def _():
                        copy = remote(src, dst, send, recv, dev)
                        copy.start() if start else copy.wait_send()
                else:
                    copy = remote(src, dst, send, recv, dev)
                    copy.start() if start else copy.wait_send()

    for r in range(1, MEMBERS):
        arrived(landing.at[lax.rem(j + MEMBERS - r, MEMBERS)], a_r.at[r])
    rows = jnp.concatenate([landing[m].astype(F32) for m in range(MEMBERS)], axis=0).astype(BF)
    wb[y, z, x] = rows[:ROWS_B]
    wc[x, z, y] = rows[ROWS_B:]

    for d in (1, 3, 2):
        push(wb.at[y, z, x], wb.at[y, z, x], row_s.at[d], row_r.at[d], (c, chip(z, y, step(x, d, NX))))
        push(wc.at[x, z, y], wc.at[x, z, y], row_s.at[4 + d], row_r.at[4 + d], (c, chip(z, step(y, d, NY), x)))
    for d in (1, 3, 2):
        arrived(wb.at[y, z, step(x, -d, NX)], row_r.at[d])
        arrived(wc.at[x, z, step(y, -d, NY)], row_r.at[4 + d])

    def chunk(part, line, zz):
        return wb.at[line, zz] if part == 0 else wc.at[line, zz]

    def half(part, line, zz, which):
        ref = wb if part == 0 else wc
        return ref.at[line, zz, pl.ds(2 * which, 2)]

    def line_device(part, d):
        if part == 0:
            return (c, chip(z, step(y, d, NY), x))
        return (c, chip(z, y, step(x, d, NX)))

    own = (y, x)
    along = (NY, NX)

    def z_sem(part, way, d):
        return (part * 2 + way) * 5 + d

    def l_sem(part, way, kind, slot):
        return ((part * 2 + way) * 2 + kind) * 8 + slot

    def z_send(part, zz, way, d):
        dev = (c, chip(step(z, 1 if way == 0 else -1, NZ), y, x))
        ref = chunk(part, own[part], zz) if d < 4 else half(part, own[part], zz, way)
        n = z_sem(part, way, d)
        push(ref, ref, z_s.at[n], z_r.at[n], dev)

    def z_wait(part, zz, way, d):
        ref = chunk(part, own[part], zz) if d < 4 else half(part, own[part], zz, way)
        arrived(ref, z_r.at[z_sem(part, way, d)])

    def line_send(part, zz, slot):
        for way, d in ((0, 1), (1, -1)):
            ref = chunk(part, own[part], zz)
            n = l_sem(part, way, 0, slot)
            push(ref, ref, l_s.at[n], l_r.at[n], line_device(part, d))

    def line_relay(part, zz, slot):
        for way, d in ((0, 1), (1, -1)):
            line = step(own[part], -d, along[part])
            arrived(chunk(part, line, zz), l_r.at[l_sem(part, way, 0, slot)])
            ref = half(part, line, zz, way)
            n = l_sem(part, way, 1, slot)
            push(ref, ref, l_s.at[n], l_r.at[n], line_device(part, d))

    def line_finish(part, zz, slot):
        for way in range(2):
            line = step(own[part], 2, along[part])
            arrived(half(part, line, zz, way), l_r.at[l_sem(part, way, 1, slot)])

    def slots(k):
        if k == 0:
            return [(z, 0)]
        if k == 4:
            return [(step(z, 4, NZ), 7)]
        return [(step(z, -k, NZ), k), (step(z, k, NZ), 3 + k)]

    def norm_rows(first, count):
        def one(n, carry):
            at = pl.multiple_of(first + n * 16, 16)
            s, row = lax.div(at, block_len), pl.multiple_of(lax.rem(at, block_len), 16)
            v = h_ref[s, pl.ds(row, 16), :].astype(F32)
            mean = jnp.mean(v * v, axis=-1, keepdims=True)
            xn[c, pl.ds(at, 16), :] = (v * lax.rsqrt(mean + EPS) * gain_ref[...]).astype(BF)
            return carry

        lax.fori_loop(0, count // 16, one, 0)

    for k in range(5):
        if k > 0:
            for way, (zz, _) in enumerate(slots(k) if k < 4 else slots(k) * 2):
                for part in range(2):
                    z_wait(part, zz, way, k)
                    if k < 4:
                        z_send(part, zz, way, k + 1)
        else:
            for way in range(2):
                for part in range(2):
                    z_send(part, z, way, 1)
        for zz, slot in slots(k):
            for part in range(2):
                line_send(part, zz, slot)
        if k == 0:
            q_pieces(True)
            norm_rows(0, 2 * block_len)
            push(xn.at[c], xn.at[c], x_s, x_r, sibling)
        if k > 0:
            for zz, slot in slots(k - 1):
                for part in range(2):
                    line_relay(part, zz, slot)
    for zz, slot in slots(4):
        for part in range(2):
            line_relay(part, zz, slot)
    for k in range(5):
        for zz, slot in slots(k):
            for part in range(2):
                line_finish(part, zz, slot)
    arrived(xn.at[1 - c], x_r)

    def project(n):
        nyl, nx = n // 2, 2 * (n % 2)
        for part_z in range(2):
            pieces = []
            for zz in range(4 * part_z, 4 * part_z + 4):
                for hi in range(2):
                    ny = 2 * hi + nyl
                    pieces.append(jnp.concatenate([wb[ny, zz, nx], wb[ny, zz, nx + 1]], axis=1))
                    pieces.append(jnp.concatenate([wc[nx, zz, ny], wc[nx + 1, zz, ny]], axis=1))
            right = jnp.concatenate(pieces, axis=0)
            depth = right.shape[0]
            for g in range(2):
                left = xn[g, :, part_z * depth:(part_z + 1) * depth]
                term = jnp.dot(left, right, preferred_element_type=F32)
                if part_z == 0:
                    acc[g] = term
                else:
                    acc[g] = acc[g] + term

    def kv_pieces(e, start):
        for k in range(8):
            q = lax.rem(i + k, 8)
            u = lax.div(q, 4) * 8 + lax.rem(lax.div(q, 2), 2) * 4 + 2 * e + lax.rem(q, 2)
            src, dst = kvs.at[u], kvb.at[SLABS + i]
            send, recv = kv_s.at[e * 8 + k], kv_r.at[SLABS + i]
            here = u == i

            @pl.when(here)
            def _():
                if start:
                    pltpu.make_async_copy(src, dst, recv).start()

            @pl.when(jnp.logical_not(here))
            def _():
                copy = remote(src, dst, send, recv, (c, z * PLANE + u))
                copy.start() if start else copy.wait_send()

    for e in range(2):
        project(e)
        for g in range(2):
            for s in range(2):
                for b in range(2):
                    head = acc[g, s * block_len:(s + 1) * block_len, b * HD:(b + 1) * HD]
                    kvs[g * 8 + s * 4 + 2 * e + b, :, :HD] = head_rotary(head, kg, cos, sin).astype(BF)
        project(2 + e)
        for g in range(2):
            for s in range(2):
                for b in range(2):
                    head = acc[g, s * block_len:(s + 1) * block_len, b * HD:(b + 1) * HD]
                    kvs[g * 8 + s * 4 + 2 * e + b, :, HD:] = head.astype(BF)
        kv_pieces(e, True)

    for n in range(SLABS):
        arrived(kvb.at[16 + n], kv_r.at[16 + n])

        @pl.when(z < NZ - 1)
        def _(n=n):
            remote(
                kvb.at[16 + n], kvb.at[n], halo_s.at[n], kv_r.at[n], (c, t + PLANE)
            ).start()
    for n in range(SLABS):
        arrived(kvb.at[8 + n], kv_r.at[8 + n])
    for n in range(PLANE):
        arrived(qb.at[n], q_r.at[n])

    unit_g = lax.div(i, 8)
    unit_s = lax.rem(lax.div(i, 4), 2)
    unit_h = c * 4 + lax.rem(i, 4)
    out_col = pl.multiple_of(unit_h * 256, 256)
    row_at = lax.broadcasted_iota(jnp.int32, (2 * HD, HD), 0)
    row_at = jnp.where(row_at >= HD, row_at - HD, row_at)
    col_at = lax.broadcasted_iota(jnp.int32, (2 * HD, HD), 1)

    def out_copy(slab):
        return remote(
            ob.at[slab], o_ref.at[unit_s, :, pl.ds(out_col, 256)],
            o_s.at[slab], o_r.at[unit_s * 8 + unit_h], (unit_g, z * PLANE + slab),
        )

    def attend(slab, first_half):
        q = jnp.concatenate([qb[slab, :, :HD], qb[slab, :, HD:]], axis=0)
        total = jnp.zeros((2 * HD, 1), F32)
        out = jnp.zeros((2 * HD, HD), F32)
        for b in range(9):
            keys = kvb[slab + b, :, :HD]
            values = kvb[slab + b, :, HD:]
            scores = lax.dot_general(q, keys, (((1,), (1,)), ((), ())), preferred_element_type=F32)
            weight = jnp.exp(scores)
            if b == 0:
                weight = jnp.where(col_at > row_at, weight, 0.0)
            if b == 8:
                weight = jnp.where(col_at <= row_at, weight, 0.0)
            elif first_half:
                seen = jnp.logical_or(z > 0, slab + b >= SLABS)
                weight = jnp.where(seen, weight, 0.0)
            total = total + jnp.sum(weight, axis=-1, keepdims=True)
            out = out + jnp.dot(weight.astype(BF), values, preferred_element_type=F32)
        out = (out / total).astype(BF)
        ob[slab] = jnp.concatenate([out[:HD], out[HD:]], axis=1)
        here = jnp.logical_and(unit_g == c, slab == i)

        @pl.when(here)
        def _():
            pltpu.make_async_copy(
                ob.at[slab], o_ref.at[unit_s, :, pl.ds(out_col, 256)], o_r.at[unit_s * 8 + unit_h]
            ).start()

        @pl.when(jnp.logical_not(here))
        def _():
            out_copy(slab).start()

    def late(n, carry):
        attend(8 + lax.rem(i + n, 8), False)
        return carry

    lax.fori_loop(0, 8, late, 0)

    for n in range(SLABS):
        @pl.when(z > 0)
        def _(n=n):
            arrived(kvb.at[n], kv_r.at[n])

        @pl.when(z == 0)
        def _(n=n):
            kvb[n] = jnp.zeros((HD, 2 * HD), BF)

    def early(n, carry):
        attend(lax.rem(i + n, 8), True)
        return carry

    lax.fori_loop(0, 8, early, 0)

    for s in range(2):
        for h in range(8):
            arrived(o_ref.at[s, :, pl.ds(h * 256, 256)], o_r.at[s * 8 + h])

    for copy in pending:
        copy.wait_send()
    q_pieces(False)
    kv_pieces(0, False)
    kv_pieces(1, False)
    for n in range(SLABS):
        @pl.when(z < NZ - 1)
        def _(n=n):
            remote(
                kvb.at[16 + n], kvb.at[n], halo_s.at[n], kv_r.at[n], (c, t + PLANE)
            ).wait_send()
    for slab in range(PLANE):
        @pl.when(jnp.logical_not(jnp.logical_and(unit_g == c, slab == i)))
        def _(slab=slab):
            out_copy(slab).wait_send()


def body(hidden, queries, input_gain, kv_weight, query_gain, key_gain):
    block_len = hidden.shape[1]
    model_width = hidden.shape[2]
    positions = lax.axis_index("ctx") * block_len + jnp.arange(block_len, dtype=jnp.int32)
    exponent = 2.0 * jnp.arange(HD // 2, dtype=F32) / HD
    inverse = jnp.power(10000.0, -exponent)
    angles = positions.astype(F32)[:, None] * inverse[None, :]
    cos, sin = jnp.cos(angles), jnp.sin(angles)
    cos = jnp.concatenate([cos, cos], axis=1)
    sin = jnp.concatenate([-sin, sin], axis=1)
    dma = pltpu.SemaphoreType.DMA
    return pl.pallas_call(
        kernel,
        out_shape=jax.ShapeDtypeStruct(queries.shape, BF),
        in_specs=[pl.BlockSpec(memory_space=pltpu.VMEM)] * 8,
        out_specs=pl.BlockSpec(memory_space=pltpu.VMEM),
        scratch_shapes=[
            pltpu.VMEM((MEMBERS, 42, HD), BF),
            pltpu.VMEM((NY, NZ, NX, ROWS_B, HD), BF),
            pltpu.VMEM((NX, NZ, NY, ROWS_C, HD), BF),
            pltpu.VMEM((2, 2 * block_len, model_width), BF),
            pltpu.VMEM((2, 2 * block_len, 256), F32),
            pltpu.VMEM((16, HD, 256), BF),
            pltpu.VMEM((24, HD, 256), BF),
            pltpu.VMEM(queries.shape, BF),
            pltpu.VMEM((16, HD, 256), BF),
            pltpu.VMEM((16, HD, 256), BF),
            dma((8,)), dma((8,)), dma((8,)), dma((8,)), dma((20,)), dma((20,)),
            dma((64,)), dma((64,)), dma, dma,
            dma((16,)), dma((16,)), dma((16,)), dma((24,)), dma((8,)), dma((16,)), dma((16,)),
        ],
        compiler_params=pltpu.CompilerParams(
            collective_id=0, has_side_effects=True, vmem_limit_bytes=60 << 20
        ),
    )(
        kv_weight, hidden, queries, input_gain.reshape(1, -1),
        query_gain.reshape(1, -1), key_gain.reshape(1, -1), cos, sin,
    )


def solution(mesh):
    return jax.shard_map(
        body,
        mesh=mesh,
        in_specs=(P("dp", "ctx", None), P("dp", "ctx", None), P(), P("ctx", None), P(), P()),
        out_specs=P("dp", "ctx", None),
        check_vma=False,
    )
```

time: 530 us -> 128 us (0.24)
  the two profiles are of different devices: /device:TPU:64 before, /device:TPU:1 now
where the time goes in v1:
time: 128 us
  Pallas kernels  123 us (96%)
  local copies, waits for them, and re-layouts  3.67 us (3%)
    pallas_call x1, Pallas kernels, body(): pl.pallas_call(kernel, out_shape=jax.ShapeDtypeStruct(queries.shape, BF),...  123 us

profile of v1, /device:TPU:1, one launch (start us, length us, event | category | flops | bytes accessed | tf_op | source)
XLA Modules:
  0.0 128.1 jit_solution(9429000619893689666)
XLA Ops:
  0.0 1.4 %reshape.20.gain_ref = f32[1,5376]{1,0:T(1,128)} reshape(f32[5376]{0:T(1024)} %param.8) | data formatting | bytes 43008 | tf_op jit(solution)/shard_map/reshape | solution.py:426
  1.4 0.3 fusion
  1.7 0.8 pad_maximum_fusion
  2.4 123.4 %shard_map.64 = bf16[2,128,2048]{2,1,0:T(8,128)(2,1)} custom-call(bf16[42,2048]{1,0:T(8,128)(2,1)} %w_ref.1, bf16[2,128,5376]{2,1,0:T(8,128)(2,1)} %h_ref.1, bf16[2,128,2048]{2,1,0:T(8,128)(2,1)} %q_ref.1, f32[1,5376]{1,0:T(1,128)} %reshape.20.gain_ref, f32[1,128]{1,0:T(1,128)} %bitcast.2, f32[1,128]{1,0:T(1,128)} %bitcast.3, ...), custom_call_target="tpu_custom_call" | custom-call | tf_op jit(solution)/shard_map/pallas_call | solution.py:402
  125.8 2.3 %copy.8 = bf16[2,128,2048]{2,1,0:T(8,128)(2,1)} copy(bf16[2,128,2048]{2,1,0:T(8,128)(2,1)} %shard_map.64) | data formatting | bytes 2097152
  (2 shorter events, 0.0 us)

commit v2 on v1

--- a/solution.py
+++ b/solution.py
@@ -13,7 +13,9 @@
 PLANE = NX * NY
 SLABS = WINDOW // HD
 MEMBERS = 8
-ROWS_B, ROWS_C = 176, 160
+ROWS_A, ROWS_B, ROWS_C = 80, 128, 128
+PLANE_ROWS = 2 * (ROWS_A + ROWS_B + ROWS_C)
+PLANE_LANES = 768
 BF = jnp.bfloat16
 F32 = jnp.float32
 MESH = pl.DeviceIdType.MESH
@@ -26,9 +28,9 @@
 
 
 def kernel(
-    w_ref, h_ref, q_ref, gain_ref, qg_ref, kg_ref, cos_ref, sin_ref, o_ref,
-    landing, wb, wc, xn, acc, kvs, kvb, qn, qb, ob,
-    a_s, a_r, row_s, row_r, z_s, z_r, l_s, l_r, x_s, x_r,
+    w_hbm, h_hbm, q_hbm, gain_hbm, qg_hbm, kg_hbm, cos_hbm, sin_hbm, o_ref,
+    w_ref, gain_ref, qg_ref, kg_ref, cos_ref, sin_ref, landing, wa, wb, wc, h_ref, q_ref, xn, acc, kvs, kvb, qn, qb, ob,
+    in_s, a_s, a_r, row_s, row_r, p_s, p_r, az_s, az_r, z_s, z_r, l_s, l_r, x_s, x_r,
     q_s, q_r, kv_s, kv_r, halo_s, o_s, o_r,
 ):
     c = lax.axis_index("dp")
@@ -64,6 +66,16 @@
     def arrived(region, recv):
         pltpu.make_async_copy(region, region, recv).wait()
 
+    loads = [
+        pltpu.make_async_copy(src, dst, in_s.at[n])
+        for n, (src, dst) in enumerate((
+            (w_hbm, w_ref), (q_hbm, q_ref), (qg_hbm, qg_ref.at[0]), (kg_hbm, kg_ref.at[0]),
+            (cos_hbm, cos_ref), (sin_hbm, sin_ref), (h_hbm, h_ref), (gain_hbm, gain_ref.at[0]),
+        ))
+    ]
+    for load in loads:
+        load.start()
+
     barrier = pltpu.get_barrier_semaphore()
     for r in range(1, 2 * PLANE):
         dev = (lax.rem(c + r % 2, 2), z * PLANE + lax.rem(i + r // 2, PLANE))
@@ -73,15 +85,13 @@
             barrier, inc=1, device_id=(c, chip(step(z, d, NZ), y, x)), device_id_type=MESH
         )
 
-    cos = cos_ref[...]
-    sin = sin_ref[...]
-    qg = qg_ref[...]
-    kg = kg_ref[...]
-    for s in range(2):
+
+    def query_heads(s):
         for h in range(16):
             head = q_ref[s, :, h * HD:(h + 1) * HD].astype(F32)
             qn[s, :, h * HD:(h + 1) * HD] = (head_rotary(head, qg, cos, sin) * SCALE).astype(BF)
 
+    loads[0].wait()
     pl.semaphore_wait(barrier, 2 * PLANE - 1 + 2)
 
     j = yl * NX + x
@@ -123,15 +133,23 @@
                     copy = remote(src, dst, send, recv, dev)
                     copy.start() if start else copy.wait_send()
 
+    for load in loads[1:6]:
+        load.wait()
+    cos, sin, qg, kg = cos_ref[...], sin_ref[...], qg_ref[...], kg_ref[...]
+    query_heads(0)
     for r in range(1, MEMBERS):
         arrived(landing.at[lax.rem(j + MEMBERS - r, MEMBERS)], a_r.at[r])
     rows = jnp.concatenate([landing[m].astype(F32) for m in range(MEMBERS)], axis=0).astype(BF)
-    wb[y, z, x] = rows[:ROWS_B]
-    wc[x, z, y] = rows[ROWS_B:]
+    wa[z, x, y] = rows[:ROWS_A]
+    wb[y, z, x] = rows[ROWS_A:ROWS_A + ROWS_B]
+    wc[x, z, y] = rows[ROWS_A + ROWS_B:]
 
     for d in (1, 3, 2):
         push(wb.at[y, z, x], wb.at[y, z, x], row_s.at[d], row_r.at[d], (c, chip(z, y, step(x, d, NX))))
         push(wc.at[x, z, y], wc.at[x, z, y], row_s.at[4 + d], row_r.at[4 + d], (c, chip(z, step(y, d, NY), x)))
+    for d in (1, 3, 2):
+        push(wa.at[z, x, y], wa.at[z, x, y], row_s.at[8 + d], row_r.at[8 + d], (c, chip(z, step(y, d, NY), x)))
+    query_heads(1)
     for d in (1, 3, 2):
         arrived(wb.at[y, z, step(x, -d, NX)], row_r.at[d])
         arrived(wc.at[x, z, step(y, -d, NY)], row_r.at[4 + d])
@@ -193,16 +211,76 @@
             return [(step(z, 4, NZ), 7)]
         return [(step(z, -k, NZ), k), (step(z, k, NZ), 3 + k)]
 
-    def norm_rows(first, count):
+    def norm_rows():
         def one(n, carry):
-            at = pl.multiple_of(first + n * 16, 16)
+            at = pl.multiple_of(n * 16, 16)
             s, row = lax.div(at, block_len), pl.multiple_of(lax.rem(at, block_len), 16)
             v = h_ref[s, pl.ds(row, 16), :].astype(F32)
             mean = jnp.mean(v * v, axis=-1, keepdims=True)
-            xn[c, pl.ds(at, 16), :] = (v * lax.rsqrt(mean + EPS) * gain_ref[...]).astype(BF)
+            v = v * lax.rsqrt(mean + EPS) * gain_ref[...]
+            pad = jnp.zeros((16, PLANE_LANES - PLANE_ROWS), F32)
+            for zz in range(NZ):
+                piece = jnp.concatenate([v[:, zz * PLANE_ROWS:(zz + 1) * PLANE_ROWS], pad], axis=1)
+                xn[zz, c, pl.ds(at, 16), :] = piece.astype(BF)
             return carry
 
-        lax.fori_loop(0, count // 16, one, 0)
+        lax.fori_loop(0, 2 * block_len // 16, one, 0)
+
+    def plane_across():
+        for d in (1, 3, 2):
+            arrived(wa.at[z, x, step(y, -d, NY)], row_r.at[8 + d])
+        for d in (1, 3, 2):
+            push(wa.at[z, x], wa.at[z, x], p_s.at[d], p_r.at[d], (c, chip(z, y, step(x, d, NX))))
+
+    def plane_send(zz, way, d):
+        dev = (c, chip(step(z, 1 if way == 0 else -1, NZ), y, x))
+        for which in range(2):
+            if d < 4 or which == way:
+                ref = wa.at[zz, pl.ds(2 * which, 2)]
+                n = (way * 2 + which) * 5 + d
+                push(ref, ref, az_s.at[n], az_r.at[n], dev)
+
+    def plane_relay(k):
+        if k == 0:
+            for d in (1, 3, 2):
+                arrived(wa.at[z, step(x, -d, NX)], p_r.at[d])
+            plane_send(z, 0, 1)
+            plane_send(z, 1, 1)
+            return
+        dev = [(c, chip(step(z, 1 if way == 0 else -1, NZ), y, x)) for way in range(2)]
+        for which in range(2):
+            for way in range(2):
+                zz = step(z, -k if way == 0 else k, NZ)
+                if k == 4 and which != way:
+                    continue
+                ref = wa.at[zz, pl.ds(2 * which, 2)]
+                n = (way * 2 + which) * 5 + k
+                arrived(ref, az_r.at[n])
+                if k < 3 or (k == 3 and which == way):
+                    push(ref, ref, az_s.at[n + 1], az_r.at[n + 1], dev[way])
+
+    def project(zz, first):
+        def pair(n, carry):
+            nyl, nx = lax.div(n, 2), 2 * lax.rem(n, 2)
+            pieces = []
+            for hi in range(2):
+                ny = 2 * hi + nyl
+                pieces.append(jnp.concatenate([wa[zz, nx, ny], wa[zz, nx + 1, ny]], axis=1))
+                pieces.append(jnp.concatenate([wb[ny, zz, nx], wb[ny, zz, nx + 1]], axis=1))
+                pieces.append(jnp.concatenate([wc[nx, zz, ny], wc[nx + 1, zz, ny]], axis=1))
+            right = jnp.concatenate(pieces, axis=0)
+            for g in range(2):
+                term = jnp.dot(xn[zz, g, :, :PLANE_ROWS], right, preferred_element_type=F32)
+                acc[n, g] = term if first else acc[n, g] + term
+            return carry
+
+        lax.fori_loop(0, 4, pair, 0)
+
+    def complete(k):
+        for zz, slot in slots(k):
+            for part in range(2):
+                line_finish(part, zz, slot)
+            project(zz, k == 0)
 
     for k in range(5):
         if k > 0:
@@ -218,41 +296,32 @@
         for zz, slot in slots(k):
             for part in range(2):
                 line_send(part, zz, slot)
+        if k == 1:
+            plane_relay(0)
         if k == 0:
+            plane_across()
             q_pieces(True)
-            norm_rows(0, 2 * block_len)
-            push(xn.at[c], xn.at[c], x_s, x_r, sibling)
+            for load in loads[6:]:
+                load.wait()
+            norm_rows()
+            push(xn.at[:, c], xn.at[:, c], x_s, x_r, sibling)
         if k > 0:
             for zz, slot in slots(k - 1):
                 for part in range(2):
                     line_relay(part, zz, slot)
+            if k > 1:
+                plane_relay(k - 1)
+        if k == 3:
+            arrived(xn.at[:, 1 - c], x_r)
+        if k > 2:
+            complete(k - 3)
     for zz, slot in slots(4):
         for part in range(2):
             line_relay(part, zz, slot)
-    for k in range(5):
-        for zz, slot in slots(k):
-            for part in range(2):
-                line_finish(part, zz, slot)
-    arrived(xn.at[1 - c], x_r)
-
-    def project(n):
-        nyl, nx = n // 2, 2 * (n % 2)
-        for part_z in range(2):
-            pieces = []
-            for zz in range(4 * part_z, 4 * part_z + 4):
-                for hi in range(2):
-                    ny = 2 * hi + nyl
-                    pieces.append(jnp.concatenate([wb[ny, zz, nx], wb[ny, zz, nx + 1]], axis=1))
-                    pieces.append(jnp.concatenate([wc[nx, zz, ny], wc[nx + 1, zz, ny]], axis=1))
-            right = jnp.concatenate(pieces, axis=0)
-            depth = right.shape[0]
-            for g in range(2):
-                left = xn[g, :, part_z * depth:(part_z + 1) * depth]
-                term = jnp.dot(left, right, preferred_element_type=F32)
-                if part_z == 0:
-                    acc[g] = term
-                else:
-                    acc[g] = acc[g] + term
+    complete(2)
+    complete(3)
+    plane_relay(4)
+    complete(4)
 
     def kv_pieces(e, start):
         for k in range(8):
@@ -273,17 +342,15 @@
                 copy.start() if start else copy.wait_send()
 
     for e in range(2):
-        project(e)
         for g in range(2):
             for s in range(2):
                 for b in range(2):
-                    head = acc[g, s * block_len:(s + 1) * block_len, b * HD:(b + 1) * HD]
+                    head = acc[e, g, s * block_len:(s + 1) * block_len, b * HD:(b + 1) * HD]
                     kvs[g * 8 + s * 4 + 2 * e + b, :, :HD] = head_rotary(head, kg, cos, sin).astype(BF)
-        project(2 + e)
         for g in range(2):
             for s in range(2):
                 for b in range(2):
-                    head = acc[g, s * block_len:(s + 1) * block_len, b * HD:(b + 1) * HD]
+                    head = acc[2 + e, g, s * block_len:(s + 1) * block_len, b * HD:(b + 1) * HD]
                     kvs[g * 8 + s * 4 + 2 * e + b, :, HD:] = head.astype(BF)
         kv_pieces(e, True)
 
@@ -401,21 +468,33 @@
     dma = pltpu.SemaphoreType.DMA
     return pl.pallas_call(
         kernel,
-        out_shape=jax.ShapeDtypeStruct(queries.shape, BF),
-        in_specs=[pl.BlockSpec(memory_space=pltpu.VMEM)] * 8,
+        out_shape=pltpu.VMEM(queries.shape, BF),
+        in_specs=[
+            pl.BlockSpec(memory_space=pl.ANY) for n in range(8)
+        ],
         out_specs=pl.BlockSpec(memory_space=pltpu.VMEM),
         scratch_shapes=[
+            pltpu.VMEM(kv_weight.shape, BF),
+            pltpu.VMEM((1, model_width), F32),
+            pltpu.VMEM((1, HD), F32),
+            pltpu.VMEM((1, HD), F32),
+            pltpu.VMEM((block_len, HD), F32),
+            pltpu.VMEM((block_len, HD), F32),
             pltpu.VMEM((MEMBERS, 42, HD), BF),
+            pltpu.VMEM((NZ, NX, NY, ROWS_A, HD), BF),
             pltpu.VMEM((NY, NZ, NX, ROWS_B, HD), BF),
             pltpu.VMEM((NX, NZ, NY, ROWS_C, HD), BF),
-            pltpu.VMEM((2, 2 * block_len, model_width), BF),
-            pltpu.VMEM((2, 2 * block_len, 256), F32),
+            pltpu.VMEM(hidden.shape, BF),
+            pltpu.VMEM(queries.shape, BF),
+            pltpu.VMEM((NZ, 2, 2 * block_len, PLANE_LANES), BF),
+            pltpu.VMEM((4, 2, 2 * block_len, 256), F32),
             pltpu.VMEM((16, HD, 256), BF),
             pltpu.VMEM((24, HD, 256), BF),
             pltpu.VMEM(queries.shape, BF),
             pltpu.VMEM((16, HD, 256), BF),
             pltpu.VMEM((16, HD, 256), BF),
-            dma((8,)), dma((8,)), dma((8,)), dma((8,)), dma((20,)), dma((20,)),
+            dma((8,)), dma((8,)), dma((8,)), dma((12,)), dma((12,)), dma((4,)), dma((4,)),
+            dma((20,)), dma((20,)), dma((20,)), dma((20,)),
             dma((64,)), dma((64,)), dma, dma,
             dma((16,)), dma((16,)), dma((16,)), dma((24,)), dma((8,)), dma((16,)), dma((16,)),
         ],
@@ -423,8 +502,7 @@
             collective_id=0, has_side_effects=True, vmem_limit_bytes=60 << 20
         ),
     )(
-        kv_weight, hidden, queries, input_gain.reshape(1, -1),
-        query_gain.reshape(1, -1), key_gain.reshape(1, -1), cos, sin,
+        kv_weight, hidden, queries, input_gain, query_gain, key_gain, cos, sin,
     )
 
 

time: 128 us -> 110 us (0.86)
  Pallas kernels: 123 us -> 108 us
  local copies, waits for them, and re-layouts: 3.67 us -> 0.97 us
    pallas_call x1, Pallas kernels: 123 us -> 108 us  [body(): pl.pallas_call(kernel, out_shape=pltpu.VMEM(queries.shape, BF), in_specs=...]
    reshape x1 -> x0, local copies, waits for them, and re-layouts: 1.36 us -> none  [body(): input_gain.reshape(1, -1)]
    unnamed x1, local copies, waits for them, and re-layouts: 2.3 us -> 0.97 us
where the time goes in v2:
time: 110 us
  Pallas kernels  108 us (98%)
    pallas_call x1, Pallas kernels, body(): pl.pallas_call(kernel, out_shape=pltpu.VMEM(queries.shape, BF), in_specs=...  108 us

profile of v2, /device:TPU:1, one launch (start us, length us, event | category | flops | bytes accessed | tf_op | source)
XLA Modules:
  0.0 109.9 jit_solution(3672447514832463455)
XLA Ops:
  0.0 0.3 fusion
  0.3 0.7 pad_maximum_fusion
  1.1 107.8 %shard_map.64 = bf16[2,128,2048]{2,1,0:T(8,128)(2,1)S(1)} custom-call(bf16[42,2048]{1,0:T(8,128)(2,1)} %w_hbm.1, bf16[2,128,5376]{2,1,0:T(8,128)(2,1)} %h_hbm.1, bf16[2,128,2048]{2,1,0:T(8,128)(2,1)} %q_hbm.1, f32[5376]{0:T(1024)} %gain_hbm.1, f32[128]{0:T(128)} %qg_hbm.1, f32[128]{0:T(128)} %kg_hbm.1, f32[128,128]{1,0:T(8,128)} %get-tuple-element.8.cos_hbm, ...), custom_call_target="tpu_custom_call" | custom-call | tf_op jit(solution)/shard_map/pallas_call | solution.py:469
  108.9 1.0 copy.8
  (2 shorter events, 0.0 us)

commit v3 on v2

--- a/solution.py
+++ b/solution.py
@@ -259,19 +259,26 @@
                 if k < 3 or (k == 3 and which == way):
                     push(ref, ref, az_s.at[n + 1], az_r.at[n + 1], dev[way])
 
-    def project(zz, first):
+    def rows_of(zz, nyl, nx):
+        pieces = []
+        for hi in range(2):
+            ny = 2 * hi + nyl
+            pieces.append(jnp.concatenate([wa[zz, nx, ny], wa[zz, nx + 1, ny]], axis=1))
+            pieces.append(jnp.concatenate([wb[ny, zz, nx], wb[ny, zz, nx + 1]], axis=1))
+            pieces.append(jnp.concatenate([wc[nx, zz, ny], wc[nx + 1, zz, ny]], axis=1))
+        return jnp.concatenate(pieces, axis=0)
+
+    def project(planes, first):
         def pair(n, carry):
             nyl, nx = lax.div(n, 2), 2 * lax.rem(n, 2)
-            pieces = []
-            for hi in range(2):
-                ny = 2 * hi + nyl
-                pieces.append(jnp.concatenate([wa[zz, nx, ny], wa[zz, nx + 1, ny]], axis=1))
-                pieces.append(jnp.concatenate([wb[ny, zz, nx], wb[ny, zz, nx + 1]], axis=1))
-                pieces.append(jnp.concatenate([wc[nx, zz, ny], wc[nx + 1, zz, ny]], axis=1))
-            right = jnp.concatenate(pieces, axis=0)
             for g in range(2):
-                term = jnp.dot(xn[zz, g, :, :PLANE_ROWS], right, preferred_element_type=F32)
-                acc[n, g] = term if first else acc[n, g] + term
+                term = None if first else acc[n, g]
+                for zz in planes:
+                    more = jnp.dot(
+                        xn[zz, g, :, :PLANE_ROWS], rows_of(zz, nyl, nx), preferred_element_type=F32
+                    )
+                    term = more if term is None else term + more
+                acc[n, g] = term
             return carry
 
         lax.fori_loop(0, 4, pair, 0)
@@ -280,7 +287,7 @@
         for zz, slot in slots(k):
             for part in range(2):
                 line_finish(part, zz, slot)
-            project(zz, k == 0)
+        project([zz for zz, _ in slots(k)], k == 0)
 
     for k in range(5):
         if k > 0:
@@ -323,47 +330,41 @@
     plane_relay(4)
     complete(4)
 
-    def kv_pieces(e, start):
-        for k in range(8):
-            q = lax.rem(i + k, 8)
-            u = lax.div(q, 4) * 8 + lax.rem(lax.div(q, 2), 2) * 4 + 2 * e + lax.rem(q, 2)
+    def kv_pieces(start):
+        for k in range(PLANE):
+            u = lax.rem(i + k, PLANE)
             src, dst = kvs.at[u], kvb.at[SLABS + i]
-            send, recv = kv_s.at[e * 8 + k], kv_r.at[SLABS + i]
-            here = u == i
-
-            @pl.when(here)
-            def _():
-                if start:
-                    pltpu.make_async_copy(src, dst, recv).start()
-
-            @pl.when(jnp.logical_not(here))
-            def _():
+            send, recv = kv_s.at[k], kv_r.at[SLABS + i]
+            if k > 0:
                 copy = remote(src, dst, send, recv, (c, z * PLANE + u))
                 copy.start() if start else copy.wait_send()
-
-    for e in range(2):
-        for g in range(2):
-            for s in range(2):
-                for b in range(2):
-                    head = acc[e, g, s * block_len:(s + 1) * block_len, b * HD:(b + 1) * HD]
-                    kvs[g * 8 + s * 4 + 2 * e + b, :, :HD] = head_rotary(head, kg, cos, sin).astype(BF)
-        for g in range(2):
-            for s in range(2):
-                for b in range(2):
-                    head = acc[2 + e, g, s * block_len:(s + 1) * block_len, b * HD:(b + 1) * HD]
-                    kvs[g * 8 + s * 4 + 2 * e + b, :, HD:] = head.astype(BF)
-        kv_pieces(e, True)
-
-    for n in range(SLABS):
-        arrived(kvb.at[16 + n], kv_r.at[16 + n])
-
-        @pl.when(z < NZ - 1)
-        def _(n=n):
-            remote(
-                kvb.at[16 + n], kvb.at[n], halo_s.at[n], kv_r.at[n], (c, t + PLANE)
-            ).start()
-    for n in range(SLABS):
-        arrived(kvb.at[8 + n], kv_r.at[8 + n])
+            elif start:
+                pltpu.make_async_copy(src, dst, recv).start()
+
+    for g in range(2):
+        for s in range(2):
+            for h in range(4):
+                rows, lanes = slice(s * block_len, (s + 1) * block_len), slice(h % 2 * HD, (h % 2 + 1) * HD)
+                u = g * 8 + s * 4 + h
+                kvs[u, :, :HD] = head_rotary(acc[h // 2, g, rows, lanes], kg, cos, sin).astype(BF)
+                kvs[u, :, HD:] = acc[2 + h // 2, g, rows, lanes].astype(BF)
+    kv_pieces(True)
+
+    def halo(src):
+        n = src - SLABS
+        return remote(kvb.at[16 + n], kvb.at[n], halo_s.at[n], kv_r.at[n], (c, t + PLANE))
+
+    def receive(k, carry):
+        src = lax.rem(i + PLANE - k, PLANE)
+        arrived(kvb.at[SLABS + src], kv_r.at[SLABS + src])
+
+        @pl.when(jnp.logical_and(src >= SLABS, z < NZ - 1))
+        def _():
+            halo(src).start()
+
+        return carry
+
+    lax.fori_loop(0, PLANE, receive, 0)
     for n in range(PLANE):
         arrived(qb.at[n], q_r.at[n])
 
@@ -441,14 +442,11 @@
     for copy in pending:
         copy.wait_send()
     q_pieces(False)
-    kv_pieces(0, False)
-    kv_pieces(1, False)
+    kv_pieces(False)
     for n in range(SLABS):
         @pl.when(z < NZ - 1)
         def _(n=n):
-            remote(
-                kvb.at[16 + n], kvb.at[n], halo_s.at[n], kv_r.at[n], (c, t + PLANE)
-            ).wait_send()
+            halo(SLABS + n).wait_send()
     for slab in range(PLANE):
         @pl.when(jnp.logical_not(jnp.logical_and(unit_g == c, slab == i)))
         def _(slab=slab):

time: 110 us -> 107 us (0.973)
  Pallas kernels: 108 us -> 105 us
    pallas_call x1, Pallas kernels: 108 us -> 105 us  [body(): pl.pallas_call(kernel, out_shape=pltpu.VMEM(queries.shape, BF), in_specs=...]
where the time goes in v3:
time: 107 us
  Pallas kernels  105 us (98%)
  other arithmetic  1.07 us (1%)
    pallas_call x1, Pallas kernels, body(): pl.pallas_call(kernel, out_shape=pltpu.VMEM(queries.shape, BF), in_specs=...  105 us

profile of v3, /device:TPU:1, one launch (start us, length us, event | category | flops | bytes accessed | tf_op | source)
XLA Modules:
  0.0 107.1 jit_solution(16986360668289990862)
XLA Ops:
  0.0 0.3 fusion
  0.3 0.7 pad_maximum_fusion
  1.1 105.0 %shard_map.64 = bf16[2,128,2048]{2,1,0:T(8,128)(2,1)S(1)} custom-call(bf16[42,2048]{1,0:T(8,128)(2,1)} %w_hbm.1, bf16[2,128,5376]{2,1,0:T(8,128)(2,1)} %h_hbm.1, bf16[2,128,2048]{2,1,0:T(8,128)(2,1)} %q_hbm.1, f32[5376]{0:T(1024)} %gain_hbm.1, f32[128]{0:T(128)} %qg_hbm.1, f32[128]{0:T(128)} %kg_hbm.1, f32[128,128]{1,0:T(8,128)} %get-tuple-element.8.cos_hbm, ...), custom_call_target="tpu_custom_call" | custom-call | tf_op jit(solution)/shard_map/pallas_call | solution.py:467
  106.1 1.0 copy.8
  (2 shorter events, 0.0 us)

commit v4 on v3

--- a/solution.py
+++ b/solution.py
@@ -1,5 +1,6 @@
 import jax
 import jax.numpy as jnp
+import numpy as np
 from jax import lax
 from jax.experimental import pallas as pl
 from jax.experimental.pallas import tpu as pltpu
@@ -28,8 +29,8 @@
 
 
 def kernel(
-    w_hbm, h_hbm, q_hbm, gain_hbm, qg_hbm, kg_hbm, cos_hbm, sin_hbm, o_ref,
-    w_ref, gain_ref, qg_ref, kg_ref, cos_ref, sin_ref, landing, wa, wb, wc, h_ref, q_ref, xn, acc, kvs, kvb, qn, qb, ob,
+    w_hbm, h_hbm, q_hbm, gain_hbm, qg_hbm, kg_hbm, freq_hbm, o_ref,
+    w_ref, gain_ref, qg_ref, kg_ref, freq_ref, landing, wa, wb, wc, h_ref, q_ref, xn, acc, kvs, kvb, qn, qb, ob,
     in_s, a_s, a_r, row_s, row_r, p_s, p_r, az_s, az_r, z_s, z_r, l_s, l_r, x_s, x_r,
     q_s, q_r, kv_s, kv_r, halo_s, o_s, o_r,
 ):
@@ -41,7 +42,7 @@
     x = lax.rem(i, NX)
     yh = lax.div(y, 2)
     yl = lax.rem(y, 2)
-    block_len = cos_ref.shape[0]
+    block_len = h_ref.shape[1]
 
     def chip(zz, yy, xx):
         return zz * PLANE + yy * NX + xx
@@ -70,7 +71,7 @@
         pltpu.make_async_copy(src, dst, in_s.at[n])
         for n, (src, dst) in enumerate((
             (w_hbm, w_ref), (q_hbm, q_ref), (qg_hbm, qg_ref.at[0]), (kg_hbm, kg_ref.at[0]),
-            (cos_hbm, cos_ref), (sin_hbm, sin_ref), (h_hbm, h_ref), (gain_hbm, gain_ref.at[0]),
+            (freq_hbm, freq_ref), (h_hbm, h_ref), (gain_hbm, gain_ref.at[0]),
         ))
     ]
     for load in loads:
@@ -91,6 +92,12 @@
             head = q_ref[s, :, h * HD:(h + 1) * HD].astype(F32)
             qn[s, :, h * HD:(h + 1) * HD] = (head_rotary(head, qg, cos, sin) * SCALE).astype(BF)
 
+    loads[4].wait()
+    token = lax.broadcasted_iota(jnp.int32, (block_len, HD), 0) + t * block_len
+    angle = token.astype(F32) * freq_ref[...]
+    lane = lax.broadcasted_iota(jnp.int32, (block_len, HD), 1)
+    cos = jnp.cos(angle)
+    sin = jnp.where(lane < HD // 2, -jnp.sin(angle), jnp.sin(angle))
     loads[0].wait()
     pl.semaphore_wait(barrier, 2 * PLANE - 1 + 2)
 
@@ -133,9 +140,9 @@
                     copy = remote(src, dst, send, recv, dev)
                     copy.start() if start else copy.wait_send()
 
-    for load in loads[1:6]:
+    for load in loads[1:4]:
         load.wait()
-    cos, sin, qg, kg = cos_ref[...], sin_ref[...], qg_ref[...], kg_ref[...]
+    qg, kg = qg_ref[...], kg_ref[...]
     query_heads(0)
     for r in range(1, MEMBERS):
         arrived(landing.at[lax.rem(j + MEMBERS - r, MEMBERS)], a_r.at[r])
@@ -303,12 +310,10 @@
         for zz, slot in slots(k):
             for part in range(2):
                 line_send(part, zz, slot)
-        if k == 1:
-            plane_relay(0)
         if k == 0:
             plane_across()
             q_pieces(True)
-            for load in loads[6:]:
+            for load in loads[5:]:
                 load.wait()
             norm_rows()
             push(xn.at[:, c], xn.at[:, c], x_s, x_r, sibling)
@@ -316,6 +321,8 @@
             for zz, slot in slots(k - 1):
                 for part in range(2):
                     line_relay(part, zz, slot)
+            if k == 1:
+                plane_relay(0)
             if k > 1:
                 plane_relay(k - 1)
         if k == 3:
@@ -456,19 +463,14 @@
 def body(hidden, queries, input_gain, kv_weight, query_gain, key_gain):
     block_len = hidden.shape[1]
     model_width = hidden.shape[2]
-    positions = lax.axis_index("ctx") * block_len + jnp.arange(block_len, dtype=jnp.int32)
-    exponent = 2.0 * jnp.arange(HD // 2, dtype=F32) / HD
-    inverse = jnp.power(10000.0, -exponent)
-    angles = positions.astype(F32)[:, None] * inverse[None, :]
-    cos, sin = jnp.cos(angles), jnp.sin(angles)
-    cos = jnp.concatenate([cos, cos], axis=1)
-    sin = jnp.concatenate([-sin, sin], axis=1)
+    inverse = 10000.0 ** (-2.0 * np.arange(HD // 2) / HD)
+    freq = jnp.asarray(np.concatenate([inverse, inverse])[None, :].astype(np.float32))
     dma = pltpu.SemaphoreType.DMA
     return pl.pallas_call(
         kernel,
         out_shape=pltpu.VMEM(queries.shape, BF),
         in_specs=[
-            pl.BlockSpec(memory_space=pl.ANY) for n in range(8)
+            pl.BlockSpec(memory_space=pl.ANY) for n in range(7)
         ],
         out_specs=pl.BlockSpec(memory_space=pltpu.VMEM),
         scratch_shapes=[
@@ -476,8 +478,7 @@
             pltpu.VMEM((1, model_width), F32),
             pltpu.VMEM((1, HD), F32),
             pltpu.VMEM((1, HD), F32),
-            pltpu.VMEM((block_len, HD), F32),
-            pltpu.VMEM((block_len, HD), F32),
+            pltpu.VMEM((1, HD), F32),
             pltpu.VMEM((MEMBERS, 42, HD), BF),
             pltpu.VMEM((NZ, NX, NY, ROWS_A, HD), BF),
             pltpu.VMEM((NY, NZ, NX, ROWS_B, HD), BF),
@@ -500,7 +501,7 @@
             collective_id=0, has_side_effects=True, vmem_limit_bytes=60 << 20
         ),
     )(
-        kv_weight, hidden, queries, input_gain, query_gain, key_gain, cos, sin,
+        kv_weight, hidden, queries, input_gain, query_gain, key_gain, freq,
     )
 
 

time: 107 us -> 106 us (level)
  other arithmetic: 1.07 us -> 0 us
where the time goes in v4:
time: 106 us
  Pallas kernels  105 us (99%)
    pallas_call x1, Pallas kernels, body(): pl.pallas_call(kernel, out_shape=pltpu.VMEM(queries.shape, BF), in_specs=...  105 us

profile of v4, /device:TPU:1, one launch (start us, length us, event | category | flops | bytes accessed | tf_op | source)
XLA Modules:
  0.0 106.0 jit_solution(6132919382081609774)
XLA Ops:
  0.0 105.0 %shard_map.73 = bf16[2,128,2048]{2,1,0:T(8,128)(2,1)S(1)} custom-call(bf16[42,2048]{1,0:T(8,128)(2,1)} %w_hbm.1, bf16[2,128,5376]{2,1,0:T(8,128)(2,1)} %h_hbm.1, bf16[2,128,2048]{2,1,0:T(8,128)(2,1)} %q_hbm.1, f32[5376]{0:T(1024)} %gain_hbm.1, f32[128]{0:T(128)} %qg_hbm.1, f32[128]{0:T(128)} %kg_hbm.1, f32[1,128]{1,0:T(1,128)} %constant.2.clone.freq_hbm), custom_call_target="tpu_custom_call" | custom-call | tf_op jit(solution)/shard_map/pallas_call | solution.py:469
  105.0 1.0 copy.9
